TPU v7x, 32 devices: a whole 2x2x4 slice. The times are simulated.
32 devices in a mesh: branch: 2 (over y), res: 16 (over z, x, core).
Axes of the slice: x: 2, y: 2, z: 4, core: 2. Of those that a mesh axis runs over, the one named last changes fastest.
Arguments:
- alignment_representation: float32 [128, 96, 256], P(None, 'res'), may hold values from -6 to 6
- pairwise_state: float32 [96, 96, 128], P('res'), may hold values from -6 to 6
- alignment_mask: int32 [128, 96], P(None, 'res'), may hold values from 0 to 1, as said below
- residue_present_mask: int32 [96], P('res'), may hold values from 0 to 1, as said below
- row_projection_weight: float32 [4, 256, 256], replicated
- lateral_result_coeffs: float32 [256, 256], replicated, may hold values from -1.5 to 1.5
- pair_bias_weight: float32 [128, 8], replicated, may hold values from -0.75 to 0.75
- first_operand_coeffs: float32 [256, 32], replicated, may hold values from -0.375 to 0.375
- other_operand_coeffs: float32 [256, 32], replicated, may hold values from -0.375 to 0.375
- outer_output_weight: float32 [1024, 128], replicated, may hold values from -2 to 2
- starting_projection_weight: float32 [4, 128, 128], replicated
- starting_bias_weight: float32 [128, 4], replicated, may hold values from -0.75 to 0.75
- starting_output_weight: float32 [128, 128], replicated, may hold values from -2 to 2
- ending_projection_weight: float32 [4, 128, 128], replicated
- ending_bias_weight: float32 [128, 4], replicated, may hold values from -0.75 to 0.75
- ending_output_weight: float32 [128, 128], replicated, may hold values from -2 to 2
Outputs:
- alignment_output: float32 [128, 96, 256], P('branch', 'res')
- pairwise_output: float32 [96, 96, 128], P('res', None, 'branch')
Inputs may be any that keep to these rules, and one draw needn't show every extreme that they name: residue_present_mask is 1 on the first L residues and 0 on the rest, for a drawn L from 48 to 96. alignment_mask[s, r] is 1 exactly where s is below a drawn count from 32 to 128 and residue_present_mask[r] is 1.
All inputs are finite; a program needn't handle non-finite values.
Results may differ from a plain program's by a relative error of at most 0.0003.
Values sent between devices are 32-bit elements; how exact they have to be, the bound alone decides.
A program may use at most 128 MiB of HBM per device.

v0:
```python
import math
import jax
import jax.numpy as jnp
from jax import lax
from jax.sharding import PartitionSpec as P

ATTEND_HEADS = 8
HEADS_Z = 4
highest = lax.Precision.HIGHEST
epsilon = 1e-05
masked_score = -1000000000.0


def spread(value, axis, root):
    mine = lax.axis_index(axis) == root
    return lax.psum(jnp.where(mine, value, jnp.zeros_like(value)), axis)


def partner(block, axis, apart):
    count = lax.axis_size(axis)
    route = []
    for low in range(count):
        high = low | 1 << apart
        if high != low and high < count:
            route += [(low, high), (high, low)]
    return lax.ppermute(block, axis, route)


def layer_normalize(values):
    centred = values - jnp.mean(values, axis=-1, keepdims=True)
    variance = jnp.mean(centred * centred, axis=-1, keepdims=True)
    return centred * lax.rsqrt(variance + epsilon)


def linear_project(values, weight):
    return jnp.dot(values, weight, precision=highest, preferred_element_type=jnp.float32)


def attend(query_matrix, key_matrix, value_matrix, gate_matrix, score_bias, live_keys, head_count):
    head_width = query_matrix.shape[-1] // head_count
    shaped_q = query_matrix.reshape(query_matrix.shape[0], head_count, head_width)
    shaped_k = key_matrix.reshape(key_matrix.shape[0], head_count, head_width)
    shaped_v = value_matrix.reshape(value_matrix.shape[0], head_count, head_width)
    scores = (
        jnp.einsum("qhd,khd->hqk", shaped_q, shaped_k, precision=highest) / math.sqrt(head_width)
        + score_bias
    )
    scores = jnp.where(live_keys[None, None, :], scores, masked_score)
    scores = scores - jnp.max(scores, axis=-1, keepdims=True)
    weights = jnp.exp(scores)
    weights = weights / jnp.sum(weights, axis=-1, keepdims=True)
    mixture = jnp.einsum("hqk,khd->qhd", weights, shaped_v, precision=highest)
    return jax.nn.sigmoid(gate_matrix) * mixture.reshape(
        query_matrix.shape[0], head_count * head_width
    )


def factor_matrix(normed, float_mask, weight):
    return jnp.transpose(linear_project(normed, weight) * float_mask[:, :, None], (1, 2, 0))


def outer_block(left_matrix, mask_rows, right_all, mask_all, out_weight):
    residues, factor_width, sequences = right_all.shape

    def outer_one_row(operands):
        row_left, row_mask = operands
        outer_sum = jnp.einsum("cs,jes->jce", row_left, right_all, precision=highest)
        outer_sum = outer_sum.reshape(residues, factor_width * factor_width)
        intersection = jnp.einsum("ns,s->n", mask_all, row_mask, precision=highest)
        return linear_project(outer_sum, out_weight) / jnp.maximum(intersection, 1.0)[:, None]

    return lax.map(outer_one_row, (left_matrix, mask_rows))


def per_device(
    alignment_representation,
    pairwise_state,
    alignment_mask,
    residue_present_mask,
    row_projection_weight,
    lateral_result_coeffs,
    pair_bias_weight,
    first_operand_coeffs,
    other_operand_coeffs,
    outer_output_weight,
    starting_projection_weight,
    starting_bias_weight,
    starting_output_weight,
    ending_projection_weight,
    ending_bias_weight,
    ending_output_weight,
):
    alignment_present_flag = lax.axis_index("branch") == 0
    sequence_count = alignment_representation.shape[0]
    local_matrix = alignment_representation.shape[1]
    residues = pairwise_state.shape[1]
    pair_width = pairwise_state.shape[2]
    float_mask = alignment_mask.astype(jnp.float32)
    mask_rows = jnp.transpose(float_mask)
    update_dimensions = (local_matrix, residues, pair_width)

    def bias_rows_of(field):
        return jnp.einsum(
            "ijc,ch->hij", layer_normalize(field), pair_bias_weight, precision=highest
        )

    normed_alignment = layer_normalize(alignment_representation)
    handed = lax.cond(
        alignment_present_flag,
        lambda: jnp.zeros((pair_bias_weight.shape[1], local_matrix, residues), jnp.float32),
        lambda: bias_rows_of(pairwise_state),
    )
    own_rows = spread(handed, "branch", 1)
    row_bias = lax.all_gather(own_rows, "res", axis=1, tiled=True)
    seq_normed, seq_mask = (
        lax.all_to_all(normed_alignment, "res", split_axis=0, concat_axis=1, tiled=True),
        lax.all_to_all(float_mask, "res", split_axis=0, concat_axis=1, tiled=True),
    )

    def row_attention():
        query_matrix = linear_project(seq_normed, row_projection_weight[0])
        key_matrix = linear_project(seq_normed, row_projection_weight[1])
        value_matrix = linear_project(seq_normed, row_projection_weight[2])
        gate_matrix = linear_project(seq_normed, row_projection_weight[3])
        sequence_present = seq_mask > 0.5

        def one_sequence(operands):
            return attend(
                operands[0],
                operands[1],
                operands[2],
                operands[3],
                row_bias,
                operands[4],
                ATTEND_HEADS,
            )

        gated_output = lax.map(
            one_sequence, (query_matrix, key_matrix, value_matrix, gate_matrix, sequence_present)
        )
        return linear_project(gated_output, lateral_result_coeffs)

    row_change = lax.cond(alignment_present_flag, row_attention, lambda: jnp.zeros_like(seq_normed))
    alignment_delta = lax.all_to_all(row_change, "res", split_axis=1, concat_axis=0, tiled=True)
    alignment_result = alignment_representation + alignment_delta
    left_matrix = factor_matrix(normed_alignment, float_mask, first_operand_coeffs)
    right_matrix = factor_matrix(normed_alignment, float_mask, other_operand_coeffs)
    right_all, mask_all = (
        lax.all_gather(right_matrix, "res", axis=0, tiled=True),
        lax.all_gather(mask_rows, "res", axis=0, tiled=True),
    )
    update = lax.cond(
        alignment_present_flag,
        lambda: outer_block(left_matrix, mask_rows, right_all, mask_all, outer_output_weight),
        lambda: jnp.zeros(update_dimensions, jnp.float32),
    )
    update = spread(update, "branch", 0)
    pair_one = pairwise_state + update
    normed_one = layer_normalize(pair_one)
    start_rows = jnp.einsum("ijc,ch->hij", normed_one, starting_bias_weight, precision=highest)
    start_full, live_float = (
        lax.all_gather(start_rows, "res", axis=1, tiled=True),
        lax.all_gather(residue_present_mask.astype(jnp.float32), "res", axis=0, tiled=True),
    )
    live_keys = live_float > 0.5

    def starting():
        query_matrix = linear_project(normed_one, starting_projection_weight[0])
        key_matrix = linear_project(normed_one, starting_projection_weight[1])
        value_matrix = linear_project(normed_one, starting_projection_weight[2])
        gate_matrix = linear_project(normed_one, starting_projection_weight[3])

        def starting_one_row(operands):
            return attend(
                operands[0], operands[1], operands[2], operands[3], start_full, live_keys, HEADS_Z
            )

        gated_output = lax.map(
            starting_one_row, (query_matrix, key_matrix, value_matrix, gate_matrix)
        )
        return pair_one + linear_project(gated_output, starting_output_weight)

    pairwise_second = lax.cond(alignment_present_flag, lambda: jnp.zeros_like(pair_one), starting)
    normed_two = layer_normalize(pairwise_second)
    end_rows = jnp.einsum("ijc,ch->hij", normed_two, ending_bias_weight, precision=highest)
    end_full = lax.all_gather(end_rows, "res", axis=1, tiled=True)
    end_score = jnp.transpose(end_full, (0, 2, 1))
    normed_cols = lax.all_to_all(normed_two, "res", split_axis=1, concat_axis=0, tiled=True)
    column_shape = normed_cols.shape

    def ending():
        ending_q, ending_k, ending_v, ending_g = (
            linear_project(normed_cols, ending_projection_weight[0]),
            linear_project(normed_cols, ending_projection_weight[1]),
            linear_project(normed_cols, ending_projection_weight[2]),
            linear_project(normed_cols, ending_projection_weight[3]),
        )

        def one_column(column, buffer):
            result = attend(
                lax.dynamic_index_in_dim(ending_q, column, 1, keepdims=False),
                lax.dynamic_index_in_dim(ending_k, column, 1, keepdims=False),
                lax.dynamic_index_in_dim(ending_v, column, 1, keepdims=False),
                lax.dynamic_index_in_dim(ending_g, column, 1, keepdims=False),
                end_score,
                live_keys,
                HEADS_Z,
            )
            return lax.dynamic_update_index_in_dim(buffer, result, column, 1)

        gated_cols = lax.fori_loop(0, ending_q.shape[1], one_column, jnp.zeros_like(ending_q))
        return linear_project(gated_cols, ending_output_weight)

    ending_delta = lax.cond(
        alignment_present_flag, lambda: jnp.zeros(column_shape, jnp.float32), ending
    )
    pair_delta = lax.all_to_all(ending_delta, "res", split_axis=0, concat_axis=1, tiled=True)
    pairwise_result = pairwise_second + pair_delta
    sequence_halves = sequence_count // 2
    halved_width = pair_width // 2
    selected_alignment, selected_pairwise = partner(
        (alignment_result[sequence_halves:], pairwise_result[:, :, :halved_width]), "branch", 0
    )
    closing_alignment = jnp.where(
        alignment_present_flag, alignment_result[:sequence_halves], selected_alignment
    )
    final_pairwise = jnp.where(
        alignment_present_flag, selected_pairwise, pairwise_result[:, :, halved_width:]
    )
    return (closing_alignment, final_pairwise)


def solution(mesh):
    in_specs = (
        P(None, "res", None),
        P("res", None, None),
        P(None, "res"),
        P("res"),
        P(),
        P(),
        P(),
        P(),
        P(),
        P(),
        P(),
        P(),
        P(),
        P(),
        P(),
        P(),
    )
    out_specs = (P("branch", "res", None), P("res", None, "branch"))
    return jax.shard_map(
        per_device, mesh=mesh, in_specs=in_specs, out_specs=out_specs, check_vma=False
    )
```

profile of v0, /device:TPU:0, one launch (start us, length us, event | category | flops | bytes accessed | tf_op | source)
XLA Modules:
  0.0 355.1 jit_solution(5219426426211909906)
XLA Ops:
  8.8 1.8 fusion.82
  12.4 2.9 fusion.79
  16.0 7.4 %all-to-all-start.1 = ((f32[16,8,6]{1,2,0:T(8,128)}), f32[16,8,6]{1,2,0:T(8,128)}, u32[]{:S(2)}, u32[]{:S(2)}) async-start(f32[16,8,6]{1,2,0:T(8,128)} %copy.256), calls=%async_computation.1 | async-start | bytes 131072 | tf_op jit(solution)/shard_map/all_to_all | solution.py:117
  24.8 21.9 %all-gather = f32[16,6,128]{2,1,0:T(8,128)S(1)} all-gather(f32[1,6,128]{2,1,0:T(8,128)S(1)} %get-tuple-element.724), channel_id=1, replica_groups=mesh['branch'=2,'res'=16] {'res'}, dimensions={0}, use_global_device_ids=true | all-gather | bytes 52224 | tf_op jit(solution)/shard_map/all_gather | solution.py:150
  46.7 2.2 convolution_bitcast_fusion.4
  48.9 8.9 %all-gather.3.cloned.1.call-done = f32[96,32,128]{2,1,0:T(8,128)} async-done(((f32[6,32,128]{2,1,0:T(8,128)}), f32[96,32,128]{2,1,0:T(8,128)}) %all-gather.3.cloned.1.call-update) | async-done | bytes 1572880 | tf_op jit(solution)/shard_map/all_gather | solution.py:149
  57.8 35.2 %conditional.7 = (f32[6,96,128]{2,1,0:T(8,128)}) conditional(s32[]{:T(128)} %convert_element_type.6, () %tuple.72, (f32[6,128]{1,0:T(8,128)S(1)}, f32[6,32,128]{2,1,0:T(8,128)S(1)}, f32[96,32,128]{2,1,0:T(8,128)}, f32[1024,128]{1,0:T(8,128)S(1)}, f32[16,6,128]{2,1,0:T(8,128)S(1)}) %tuple.207), branch_computations={%region_13.14_spmd, %region_14.17_spmd} | conditional | flops 302174304 | bytes 7230381 | solution.py:152
  57.8 2.4 copy.264
  60.2 32.8 %while.40 = (s32[]{:T(128)}, f32[6,96,128]{2,1,0:T(8,128)}, f32[6,32,128]{2,1,0:T(8,128)S(1)}, f32[96,32,128]{2,0,1:T(8,128)S(1)}, f32[1024,128]{1,0:T(8,128)S(1...) while((s32[]{:T(128)}, f32[6,96,128]{2,1,0:T(8,128)}, f32[6,32,128]{2,1,0:T(8,128)S(1)}, ...), condition=%wide.region_16.16_spmd, body=%wide.region_15.15_spmd.sunk | while | flops 302149728 | bytes 3786589 | solution.py:72
  60.2 3.3 convolution_bitcast_fusion.8
  65.7 3.3 convolution_bitcast_fusion.8
  71.1 3.3 convolution_bitcast_fusion.8
  76.6 3.3 convolution_bitcast_fusion.8
  82.1 3.3 convolution_bitcast_fusion.8
  87.5 3.3 convolution_bitcast_fusion.8
  94.8 31.4 %all-reduce = f32[96]{0:T(128)S(1)} all-reduce(f32[96]{0:T(128)S(1)} %convert_dynamic-update-slice_fusion), channel_id=1, replica_groups=mesh['branch'=2,'res'=16] {'res'}, use_global_device_ids=true, to_apply=%add | all-reduce | flops 96 | bytes 768
  127.7 3.8 %all-to-all-start = ((f32[128,6,256]{2,1,0:T(8,128)}), f32[128,6,256]{2,1,0:T(8,128)S(1)}, u32[]{:S(2)}, u32[]{:S(2)}) async-start(f32[128,6,256]{2,1,0:T(8,128)} %fusion.80), calls=%async_computation | async-start | bytes 2097152 | tf_op jit(solution)/shard_map/all_to_all | solution.py:116
  132.4 33.2 %all_gather.22 = f32[4,96,96]{2,0,1:T(4,128)S(1)} all-gather(f32[4,6,96]{2,0,1:T(4,128)S(1)} %convolution_bitcast_fusion.6), channel_id=1, replica_groups=mesh['branch'=2,'res'=16] {'res'}, dimensions={1}, use_global_device_ids=true | all-gather | bytes 156672 | tf_op jit(solution)/shard_map/all_gather | solution.py:162
  167.3 5.9 %all-to-all-start.3 = ((f32[6,96,128]{2,0,1:T(8,128)}), f32[6,96,128]{2,0,1:T(8,128)}, u32[]{:S(2)}, u32[]{:S(2)}) async-start(f32[6,96,128]{2,0,1:T(8,128)} %fusion.85), calls=%async_computation.3 | async-start | bytes 786432 | tf_op jit(solution)/shard_map/all_to_all | solution.py:188
  173.2 33.9 %psum.14 = f32[8,6,96]{2,0,1:T(8,128)S(1)} all-reduce(f32[8,6,96]{2,0,1:T(8,128)S(1)} %broadcast_select_fusion.1), channel_id=1, replica_groups=mesh['branch'=2,'res'=16] {'branch'}, use_global_device_ids=true, to_apply=%region_6.7 | all-reduce | flops 4608 | bytes 36864 | tf_op jit(solution)/shard_map/psum | solution.py:16
  207.2 22.8 %all_gather.18 = f32[8,96,96]{2,0,1:T(8,128)S(1)} all-gather(f32[8,6,96]{2,0,1:T(8,128)S(1)} %psum.14), channel_id=1, replica_groups=mesh['branch'=2,'res'=16] {'res'}, dimensions={1}, use_global_device_ids=true | all-gather | bytes 313344 | tf_op jit(solution)/shard_map/all_gather | solution.py:114
  231.1 53.1 %conditional.6 = (f32[8,96,256]{2,1,0:T(8,128)S(1)}) conditional(s32[]{:T(128)} %convert_element_type.6, () %tuple.68, (f32[4,256,256]{2,1,0:T(8,128)}, f32[8,16,6,256]{3,0,1,2:T(8,128)}, f32[8,16,6]{0,2,1:T(8,128)}, f32[8,96,96]{2,0,1:T(8,128)S(1)}, f32[256,256]{1,0:T(8,128)}) %tuple.209), branch_computations={%region_7.8_spmd, %region_8.13_spmd} | conditional | flops 3077209344 | bytes 19131672 | solution.py:143
  233.9 2.3 fusion.14
  236.1 2.3 fusion.16
  238.4 2.3 fusion.18
  242.0 39.1 %while.39 = (s32[]{:T(128)}, f32[8,96,256]{1,2,0:T(8,128)}, f32[8,96,256]{1,2,0:T(8,128)}, f32[8,96,256]{1,2,0:T(8,128)}, pred[8,96]{1,0:T(8,128)(4,1)S(1)}, /*i...) while((s32[]{:T(128)}, f32[8,96,256]{1,2,0:T(8,128)}, ...), condition=%wide.region_12.12_spmd, body=%wide.region_9.11_spmd.sunk | while | flops 57309696 | bytes 2539401 | solution.py:138
  281.2 3.0 fusion.20
  285.6 3.7 %all-to-all-start.2 = ((f32[8,96,256]{2,0,1:T(8,128)}), f32[8,96,256]{2,0,1:T(8,128)S(1)}, u32[]{:S(2)}, u32[]{:S(2)}) async-start(f32[8,96,256]{2,0,1:T(8,128)} %copy.260), calls=%async_computation.2 | async-start | bytes 1572864 | tf_op jit(solution)/shard_map/all_to_all | solution.py:144
  291.0 28.1 %all_gather.23 = f32[4,96,96]{2,0,1:T(4,128)S(1)} all-gather(f32[4,6,96]{2,0,1:T(4,128)S(1)} %convolution_bitcast_fusion.5), channel_id=1, replica_groups=mesh['branch'=2,'res'=16] {'res'}, dimensions={1}, use_global_device_ids=true | all-gather | bytes 156672 | tf_op jit(solution)/shard_map/all_gather | solution.py:186
  321.5 4.5 %all-to-all-start.4 = ((f32[96,6,128]{2,1,0:T(8,128)}), f32[96,6,128]{2,1,0:T(8,128)S(1)}, u32[]{:S(2)}, u32[]{:S(2)}) async-start(f32[96,6,128]{2,1,0:T(8,128)} %copy.274), calls=%async_computation.4 | async-start | bytes 786432 | tf_op jit(solution)/shard_map/all_to_all | solution.py:217
  327.1 11.0 %all-to-all-done.4 = f32[96,6,128]{2,1,0:T(8,128)S(1)} async-done(((f32[96,6,128]{2,1,0:T(8,128)}), f32[96,6,128]{2,1,0:T(8,128)S(1)}, u32[]{:S(2)}, u32[]{:S(2)}) %all-to-all-start.4) | async-done | bytes 294944 | tf_op jit(solution)/shard_map/all_to_all | solution.py:217
  339.3 8.0 %collective-permute-done.1 = f32[6,96,64]{2,1,0:T(8,128)S(1)} collective-permute-done((f32[6,96,64]{2,1,0:T(8,128)S(1)}, f32[6,96,64]{2,1,0:T(8,128)S(1)}, u32[]{:S(2)}, u32[]{:S(2)}) %collective-permute-start.1) | collective-permute-done | bytes 147488 | tf_op jit(solution)/shard_map/ppermute | solution.py:26
  (181 shorter events, 76.0 us)
Async XLA Ops:
  7.2 5.2 %copy-start = (f32[256,32]{0,1:T(8,128)S(1)}, f32[256,32]{0,1:T(8,128)}, u32[]{:S(2)}) copy-start(f32[256,32]{0,1:T(8,128)} %param.42) | copy-start | bytes 98308
  7.2 3.6 %copy-start.2 = (f32[128,6,256]{2,0,1:T(8,128)S(1)}, f32[128,6,256]{2,0,1:T(8,128)}, u32[]{:S(2)}) copy-start(f32[128,6,256]{2,0,1:T(8,128)} %param.34) | copy-start | bytes 2359300
  7.2 50.6 %all-gather.3.cloned.1.call-start = ((), (), s32[]{:S(2)}) async-start(), calls=%async_computation.5 | async-start | bytes 1671168 | tf_op jit(solution)/shard_map/all_gather | solution.py:149
  8.6 3.7 %copy-start.12 = (s32[128,6]{0,1:T(8,128)S(1)}, s32[128,6]{0,1:T(8,128)}, u32[]{:S(2)}) copy-start(s32[128,6]{0,1:T(8,128)} %param.36) | copy-start | bytes 9220
  10.8 12.7 %copy-start.17 = (u32[32]{0:T(128)S(1)}, u32[32]{0:T(128)}, u32[]{:S(2)}) copy-start(u32[32]{0:T(128)} %constant.198) | copy-start | bytes 388
  10.8 35.9 %copy-start.11 = (f32[256,32]{0,1:T(8,128)S(1)}, f32[256,32]{0,1:T(8,128)}, u32[]{:S(2)}) copy-start(f32[256,32]{0,1:T(8,128)} %param.41) | copy-start | bytes 98308
  12.4 45.4 %copy-start.1 = (f32[1024,128]{1,0:T(8,128)S(1)}, f32[1024,128]{1,0:T(8,128)}, u32[]{:S(2)}) copy-start(f32[1024,128]{1,0:T(8,128)} %param.43) | copy-start | bytes 1572868
  16.0 111.7 %all-to-all-start.1 = ((f32[16,8,6]{1,2,0:T(8,128)}), f32[16,8,6]{1,2,0:T(8,128)}, u32[]{:S(2)}, u32[]{:S(2)}) async-start(f32[16,8,6]{1,2,0:T(8,128)} %copy.256), calls=%async_computation.1 | async-start | bytes 131072 | tf_op jit(solution)/shard_map/all_to_all | solution.py:117
  23.4 102.8 %all-reduce.3.cloned.1.call-start = ((), (), s32[]{:S(2)}) async-start(), calls=%async_computation.6 | async-start | bytes 589824 | tf_op jit(solution)/shard_map/psum | solution.py:16
  57.8 36.9 %copy-start.16 = (s32[6]{0:T(128)S(1)}, s32[6]{0:T(128)}, u32[]{:S(2)}) copy-start(s32[6]{0:T(128)} %param.37) | copy-start | bytes 76
  57.8 68.4 %copy-start.3 = (f32[6,96,128]{2,1,0:T(8,128)S(1)}, f32[6,96,128]{2,1,0:T(8,128)}, u32[]{:S(2)}) copy-start(f32[6,96,128]{2,1,0:T(8,128)} %param.35) | copy-start | bytes 884740
  127.4 4.4 %copy-start.14 = (f32[128,4]{0,1:T(4,128)S(1)}, f32[128,4]{0,1:T(4,128)}, u32[]{:S(2)}) copy-start(f32[128,4]{0,1:T(4,128)} %param.45) | copy-start | bytes 6148
  127.7 37.9 %copy-start.7 = (f32[4,128,128]{2,1,0:T(8,128)S(1)}, f32[4,128,128]{2,1,0:T(8,128)}, u32[]{:S(2)}) copy-start(f32[4,128,128]{2,1,0:T(8,128)} %param.44) | copy-start | bytes 786436
  127.7 37.9 %copy-start.9 = (f32[128,128]{1,0:T(8,128)S(1)}, f32[128,128]{1,0:T(8,128)}, u32[]{:S(2)}) copy-start(f32[128,128]{1,0:T(8,128)} %param.46) | copy-start | bytes 196612
  127.7 39.6 %all-to-all-start = ((f32[128,6,256]{2,1,0:T(8,128)}), f32[128,6,256]{2,1,0:T(8,128)S(1)}, u32[]{:S(2)}, u32[]{:S(2)}) async-start(f32[128,6,256]{2,1,0:T(8,128)} %fusion.80), calls=%async_computation | async-start | bytes 2097152 | tf_op jit(solution)/shard_map/all_to_all | solution.py:116
  165.6 7.6 %copy-start.13 = (f32[128,8]{0,1:T(8,128)S(1)}, f32[128,8]{0,1:T(8,128)}, u32[]{:S(2)}) copy-start(f32[128,8]{0,1:T(8,128)} %param.40) | copy-start | bytes 12292
  167.3 118.3 %all-to-all-start.3 = ((f32[6,96,128]{2,0,1:T(8,128)}), f32[6,96,128]{2,0,1:T(8,128)}, u32[]{:S(2)}, u32[]{:S(2)}) async-start(f32[6,96,128]{2,0,1:T(8,128)} %fusion.85), calls=%async_computation.3 | async-start | bytes 786432 | tf_op jit(solution)/shard_map/all_to_all | solution.py:188
  231.1 1.5 copy-start.6
  242.0 39.2 %copy-start.8 = (f32[256,256]{1,0:T(8,128)S(1)}, f32[256,256]{1,0:T(8,128)}, u32[]{:S(2)}) copy-start(f32[256,256]{1,0:T(8,128)} %get-tuple-element.359) | copy-start | bytes 786436 | tf_op jit(solution)/shard_map/cond
  284.2 5.1 %copy-start.15 = (f32[128,4]{0,1:T(4,128)S(1)}, f32[128,4]{0,1:T(4,128)}, u32[]{:S(2)}) copy-start(f32[128,4]{0,1:T(4,128)} %param.48) | copy-start | bytes 6148
  285.6 34.6 %copy-start.10 = (f32[128,128]{1,0:T(8,128)S(1)}, f32[128,128]{1,0:T(8,128)}, u32[]{:S(2)}) copy-start(f32[128,128]{1,0:T(8,128)} %param.49) | copy-start | bytes 196612
  285.6 35.9 %all-to-all-start.2 = ((f32[8,96,256]{2,0,1:T(8,128)}), f32[8,96,256]{2,0,1:T(8,128)S(1)}, u32[]{:S(2)}, u32[]{:S(2)}) async-start(f32[8,96,256]{2,0,1:T(8,128)} %copy.260), calls=%async_computation.2 | async-start | bytes 1572864 | tf_op jit(solution)/shard_map/all_to_all | solution.py:144
  321.5 16.6 %all-to-all-start.4 = ((f32[96,6,128]{2,1,0:T(8,128)}), f32[96,6,128]{2,1,0:T(8,128)S(1)}, u32[]{:S(2)}, u32[]{:S(2)}) async-start(f32[96,6,128]{2,1,0:T(8,128)} %copy.274), calls=%async_computation.4 | async-start | bytes 786432 | tf_op jit(solution)/shard_map/all_to_all | solution.py:217
  326.1 0.9 copy-start.4
  327.0 11.5 %copy-start.5 = (f32[128,6,256]{2,0,1:T(8,128)S(1)}, f32[128,6,256]{2,0,1:T(8,128)}, u32[]{:S(2)}) copy-start(f32[128,6,256]{2,0,1:T(8,128)} %copy-done.4) | copy-start | bytes 2359300
  327.0 11.5 %collective-permute-start = (f32[64,6,256]{2,0,1:T(8,128)S(1)}, f32[64,6,256]{2,0,1:T(8,128)S(1)}, u32[]{:S(2)}, u32[]{:S(2)}) collective-permute-start(f32[64,6,256]{2,0,1:T(8,128)S(1)} %slice.53), channel_id=1, source_target_pairs={{0,16},{16,0},{1,17},{17,1},{2,18},{18,2},{3,19},{19,3},{4,20},{20... | collective-permute-start | bytes 1179656 | tf_op jit(solution)/shard_map/ppermute | solution.py:26
  338.2 9.1 %collective-permute-start.1 = (f32[6,96,64]{2,1,0:T(8,128)S(1)}, f32[6,96,64]{2,1,0:T(8,128)S(1)}, u32[]{:S(2)}, u32[]{:S(2)}) collective-permute-start(f32[6,96,64]{2,1,0:T(8,128)S(1)} %bitcast.264), channel_id=1, source_target_pairs={{0,16},{16,0},{1,17},{17,1},{2,18},{18,2},{3,19},{19,3},{4,20},{20... | collective-permute-start | bytes 442376 | tf_op jit(solution)/shard_map/ppermute | solution.py:26
Sparse Core Ops, SparseCore 0:
  15.4 42.3 all-gather.2
  94.8 21.5 all-reduce.2
where the time goes:
time: 357 us; the launch traced here: 355 us
  blocking collectives  171 us (48%)
  matrix products  59.8 us (17%)
  local copies, waits for them, and re-layouts  30.1 us (8%)
  waiting for transfers between devices  28.2 us (8%)
  starting transfers between devices  25.5 us (7%)
  other arithmetic  24.2 us (7%)
  between operations  15.1 us (4%)
    psum x1, blocking collectives, spread(): return lax.psum(jnp.where(mine, value, jnp.zeros_like(value)), axis)  33.9 us
    all_gather x1, blocking collectives, per_device(): lax.all_gather(start_rows, 'res', axis=1, tiled=True)  33.2 us
    unnamed x1, blocking collectives  31.4 us
    all_gather x1, blocking collectives, per_device(): end_full = lax.all_gather(end_rows, 'res', axis=1, tiled=True)  28.1 us
    dot_general x13, matrix products, linear_project(): jnp.dot(values, weight, precision=highest, preferred_element_type=jnp.flo...  26.3 us
    all_gather x1, blocking collectives, per_device(): row_bias = lax.all_gather(own_rows, 'res', axis=1, tiled=True)  22.8 us
    all_gather x1, blocking collectives, per_device(): lax.all_gather(mask_rows, 'res', axis=0, tiled=True)  21.9 us
    dot_general x6, matrix products, outer_one_row(): jnp.einsum('cs,jes->jce', row_left, right_all, precision=highest)  19.8 us
  transfers between devices with their start and end apart: 9, of which 4 were waited for; matrix products, arithmetic and copies ran while one was open for 29% of the time, Pallas kernels for 0%

commit v1 on v0

--- a/solution.py
+++ b/solution.py
@@ -13,7 +13,7 @@
 
 def spread(value, axis, root):
     mine = lax.axis_index(axis) == root
-    return lax.psum(jnp.where(mine, value, jnp.zeros_like(value)), axis)
+    return jnp.sum(lax.all_gather(jnp.where(mine, value, jnp.zeros_like(value)), axis), axis=0)
 
 
 def partner(block, axis, apart):

time: 357 us -> 339 us (0.950)
  waiting for transfers between devices: 28.2 us -> 19.3 us
  blocking collectives: 171 us -> 166 us
    psum x1 -> x0, blocking collectives: 33.9 us -> none  [spread(): return lax.psum(jnp.where(mine, value, jnp.zeros_like(value)), axis)]
    all_gather x0 -> x2, blocking collectives: none -> 28.8 us  [spread(): lax.all_gather(jnp.where(mine, value, jnp.zeros_like(value)), axis)]
    all_gather x1, waiting for transfers between devices: 8.92 us -> 0.02 us  [per_device(): lax.all_gather(right_matrix, 'res', axis=0, tiled=True)]
    all_gather x1, blocking collectives: 21.9 us -> 17.3 us  [per_device(): lax.all_gather(mask_rows, 'res', axis=0, tiled=True)]
  transfers between devices with their start and end apart: 9 -> 8, of which waited for: 4 -> 3; matrix products, arithmetic and copies ran while one was open for 29% -> 30% of each run, Pallas kernels for 0% -> 0%
where the time goes in v1:
time: 339 us; the launch traced here: 338 us
  blocking collectives  166 us (49%)
  matrix products  60 us (18%)
  local copies, waits for them, and re-layouts  28.4 us (8%)
  starting transfers between devices  25.9 us (8%)
  other arithmetic  22.6 us (7%)
  waiting for transfers between devices  19.3 us (6%)
  between operations  15.1 us (4%)
    unnamed x1, blocking collectives  33.9 us
    all_gather x1, blocking collectives, per_device(): lax.all_gather(start_rows, 'res', axis=1, tiled=True)  33.1 us
    all_gather x1, blocking collectives, per_device(): end_full = lax.all_gather(end_rows, 'res', axis=1, tiled=True)  29.6 us
    all_gather x2, blocking collectives, spread(): lax.all_gather(jnp.where(mine, value, jnp.zeros_like(value)), axis)  28.8 us
    dot_general x13, matrix products, linear_project(): jnp.dot(values, weight, precision=highest, preferred_element_type=jnp.flo...  26.4 us
    all_gather x1, blocking collectives, per_device(): row_bias = lax.all_gather(own_rows, 'res', axis=1, tiled=True)  22.8 us
    dot_general x6, matrix products, outer_one_row(): jnp.einsum('cs,jes->jce', row_left, right_all, precision=highest)  19.8 us
    all_gather x1, blocking collectives, per_device(): lax.all_gather(mask_rows, 'res', axis=0, tiled=True)  17.3 us
  transfers between devices with their start and end apart: 8, of which 3 were waited for; matrix products, arithmetic and copies ran while one was open for 30% of the time, Pallas kernels for 0%

profile of v1, /device:TPU:0, one launch (start us, length us, event | category | flops | bytes accessed | tf_op | source)
XLA Modules:
  0.0 337.8 jit_solution(7296347855301102511)
XLA Ops:
  8.8 1.8 fusion.82
  12.4 2.9 fusion.79
  16.0 7.4 %all-to-all-start.1 = ((f32[16,8,6]{1,2,0:T(8,128)}), f32[16,8,6]{1,2,0:T(8,128)S(1)}, u32[]{:S(2)}, u32[]{:S(2)}) async-start(f32[16,8,6]{1,2,0:T(8,128)} %copy.244), calls=%async_computation.1 | async-start | bytes 131072 | tf_op jit(solution)/shard_map/all_to_all | solution.py:117
  24.8 33.9 %all-reduce = f32[96]{0:T(128)S(1)} all-reduce(f32[96]{0:T(128)S(1)} %convert_dynamic-update-slice_fusion), channel_id=1, replica_groups=mesh['branch'=2,'res'=16] {'res'}, use_global_device_ids=true, to_apply=%add | all-reduce | flops 96 | bytes 768
  58.7 17.3 %all-gather.2 = f32[16,6,128]{2,1,0:T(8,128)S(1)} all-gather(f32[1,6,128]{2,1,0:T(8,128)S(1)} %get-tuple-element.724), channel_id=1, replica_groups=mesh['branch'=2,'res'=16] {'res'}, dimensions={0}, use_global_device_ids=true | all-gather | bytes 52224 | tf_op jit(solution)/shard_map/all_gather | solution.py:150
  76.0 2.2 convolution_bitcast_fusion.4
  78.2 35.1 %conditional.7 = (f32[6,96,128]{2,1,0:T(8,128)}) conditional(s32[]{:T(128)} %convert_element_type.6, () %tuple.72, (f32[6,128]{1,0:T(8,128)S(1)}, f32[6,32,128]{2,1,0:T(8,128)S(1)}, f32[96,32,128]{2,1,0:T(8,128)}, f32[1024,128]{1,0:T(8,128)S(1)}, f32[16,6,128]{2,1,0:T(8,128)S(1)}) %tuple.205), branch_computations={%region_13.14_spmd, %region_14.17_spmd} | conditional | flops 302174304 | bytes 7230381 | solution.py:152
  78.2 2.3 copy.252
  80.6 32.8 %while.40 = (s32[]{:T(128)}, f32[6,96,128]{2,1,0:T(8,128)}, f32[6,32,128]{2,1,0:T(8,128)S(1)}, f32[96,32,128]{2,0,1:T(8,128)S(1)}, f32[1024,128]{1,0:T(8,128)S(1...) while((s32[]{:T(128)}, f32[6,96,128]{2,1,0:T(8,128)}, f32[6,32,128]{2,1,0:T(8,128)S(1)}, ...), condition=%wide.region_16.16_spmd, body=%wide.region_15.15_spmd.sunk | while | flops 302149728 | bytes 3786589 | solution.py:72
  80.6 3.3 convolution_bitcast_fusion.8
  86.0 3.3 convolution_bitcast_fusion.8
  91.5 3.3 convolution_bitcast_fusion.8
  97.0 3.3 convolution_bitcast_fusion.8
  102.4 3.3 convolution_bitcast_fusion.8
  107.9 3.3 convolution_bitcast_fusion.8
  114.4 9.9 %all-gather.1 = f32[12,96,128]{2,1,0:T(8,128)S(1)} all-gather(f32[6,96,128]{2,1,0:T(8,128)S(1)} %broadcast_select_fusion), channel_id=3, replica_groups=mesh['branch'=2,'res'=16] {'branch'}, dimensions={0}, use_global_device_ids=true | all-gather | bytes 884736 | tf_op jit(solution)/shard_map/all_gather | solution.py:16
  124.9 4.5 %all-to-all-start = ((f32[128,6,256]{2,1,0:T(8,128)}), f32[128,6,256]{2,1,0:T(8,128)}, u32[]{:S(2)}, u32[]{:S(2)}) async-start(f32[128,6,256]{2,1,0:T(8,128)} %fusion.80), calls=%async_computation | async-start | bytes 2097152 | tf_op jit(solution)/shard_map/all_to_all | solution.py:116
  130.2 33.1 %all_gather.38 = f32[4,96,96]{2,0,1:T(4,128)S(1)} all-gather(f32[4,6,96]{2,0,1:T(4,128)S(1)} %convolution_bitcast_fusion.6), channel_id=1, replica_groups=mesh['branch'=2,'res'=16] {'res'}, dimensions={1}, use_global_device_ids=true | all-gather | bytes 156672 | tf_op jit(solution)/shard_map/all_gather | solution.py:162
  165.1 5.7 %all-to-all-start.3 = ((f32[6,96,128]{2,0,1:T(8,128)}), f32[6,96,128]{2,0,1:T(8,128)S(1)}, u32[]{:S(2)}, u32[]{:S(2)}) async-start(f32[6,96,128]{2,0,1:T(8,128)} %fusion.85), calls=%async_computation.3 | async-start | bytes 786432 | tf_op jit(solution)/shard_map/all_to_all | solution.py:188
  170.9 18.9 %all-gather = f32[16,6,96]{2,0,1:T(8,128)S(1)} all-gather(f32[8,6,96]{2,0,1:T(8,128)S(1)} %broadcast_select_fusion.1), channel_id=2, replica_groups=mesh['branch'=2,'res'=16] {'branch'}, dimensions={0}, use_global_device_ids=true | all-gather | bytes 55296 | tf_op jit(solution)/shard_map/all_gather | solution.py:16
  189.8 22.8 %all_gather.32 = f32[8,96,96]{2,0,1:T(8,128)S(1)} all-gather(f32[8,6,96]{2,0,1:T(8,128)S(1)} %bitcast_reduce_fusion), channel_id=1, replica_groups=mesh['branch'=2,'res'=16] {'res'}, dimensions={1}, use_global_device_ids=true | all-gather | bytes 313344 | tf_op jit(solution)/shard_map/all_gather | solution.py:114
  214.1 52.4 %conditional.6 = (f32[8,96,256]{2,1,0:T(8,128)S(1)}) conditional(s32[]{:T(128)} %convert_element_type.6, () %tuple.68, (f32[4,256,256]{2,1,0:T(8,128)}, f32[8,16,6,256]{3,0,1,2:T(8,128)S(1)}, f32[8,16,6]{0,2,1:T(8,128)S(1)}, f32[8,96,96]{2,0,1:T(8,128)S(1)}, f32[256,256]{1,0:T(8,128)}) %tuple.211), branch_computations={%region_7.8_spmd, %region_8.13_spmd} | conditional | flops 3077209344 | bytes 19131672 | solution.py:143
  216.9 2.3 fusion.14
  219.2 2.3 fusion.16
  221.6 2.3 fusion.18
  224.3 39.1 %while.39 = (s32[]{:T(128)}, f32[8,96,256]{1,2,0:T(8,128)}, f32[8,96,256]{1,2,0:T(8,128)}, f32[8,96,256]{1,2,0:T(8,128)}, pred[8,96]{1,0:T(8,128)(4,1)S(1)}, /*i...) while((s32[]{:T(128)}, f32[8,96,256]{1,2,0:T(8,128)}, ...), condition=%wide.region_12.12_spmd, body=%wide.region_9.11_spmd.sunk | while | flops 57309696 | bytes 2539401 | solution.py:138
  263.5 3.0 fusion.20
  267.9 3.7 %all-to-all-start.2 = ((f32[8,96,256]{2,0,1:T(8,128)}), f32[8,96,256]{2,0,1:T(8,128)S(1)}, u32[]{:S(2)}, u32[]{:S(2)}) async-start(f32[8,96,256]{2,0,1:T(8,128)} %copy.248), calls=%async_computation.2 | async-start | bytes 1572864 | tf_op jit(solution)/shard_map/all_to_all | solution.py:144
  273.3 29.6 %all_gather.39 = f32[4,96,96]{2,0,1:T(4,128)} all-gather(f32[4,6,96]{2,0,1:T(4,128)S(1)} %convolution_bitcast_fusion.5), channel_id=1, replica_groups=mesh['branch'=2,'res'=16] {'res'}, dimensions={1}, use_global_device_ids=true | all-gather | bytes 156672 | tf_op jit(solution)/shard_map/all_gather | solution.py:186
  304.3 4.4 %all-to-all-start.4 = ((f32[96,6,128]{2,1,0:T(8,128)}), f32[96,6,128]{2,1,0:T(8,128)S(1)}, u32[]{:S(2)}, u32[]{:S(2)}) async-start(f32[96,6,128]{2,1,0:T(8,128)} %copy.262), calls=%async_computation.4 | async-start | bytes 786432 | tf_op jit(solution)/shard_map/all_to_all | solution.py:217
  309.8 11.0 %all-to-all-done.4 = f32[96,6,128]{2,1,0:T(8,128)S(1)} async-done(((f32[96,6,128]{2,1,0:T(8,128)}), f32[96,6,128]{2,1,0:T(8,128)S(1)}, u32[]{:S(2)}, u32[]{:S(2)}) %all-to-all-start.4) | async-done | bytes 294944 | tf_op jit(solution)/shard_map/all_to_all | solution.py:217
  322.0 8.0 %collective-permute-done.1 = f32[6,96,64]{2,1,0:T(8,128)S(1)} collective-permute-done((f32[6,96,64]{2,1,0:T(8,128)S(1)}, f32[6,96,64]{2,1,0:T(8,128)S(1)}, u32[]{:S(2)}, u32[]{:S(2)}) %collective-permute-start.1) | collective-permute-done | bytes 147488 | tf_op jit(solution)/shard_map/ppermute | solution.py:26
  (179 shorter events, 72.7 us)
Async XLA Ops:
  7.2 5.2 %copy-start = (f32[256,32]{0,1:T(8,128)S(1)}, f32[256,32]{0,1:T(8,128)}, u32[]{:S(2)}) copy-start(f32[256,32]{0,1:T(8,128)} %param.42) | copy-start | bytes 98308
  7.2 3.6 %copy-start.2 = (f32[128,6,256]{2,0,1:T(8,128)S(1)}, f32[128,6,256]{2,0,1:T(8,128)}, u32[]{:S(2)}) copy-start(f32[128,6,256]{2,0,1:T(8,128)} %param.34) | copy-start | bytes 2359300
  7.2 71.0 %all-gather.5.cloned.1.call-start = ((), (), s32[]{:S(2)}) async-start(), calls=%async_computation.5 | async-start | bytes 1671168 | tf_op jit(solution)/shard_map/all_gather | solution.py:149
  8.6 3.8 %copy-start.12 = (s32[128,6]{0,1:T(8,128)S(1)}, s32[128,6]{0,1:T(8,128)}, u32[]{:S(2)}) copy-start(s32[128,6]{0,1:T(8,128)} %param.36) | copy-start | bytes 9220
  10.8 12.6 %copy-start.17 = (u32[32]{0:T(128)S(1)}, u32[32]{0:T(128)}, u32[]{:S(2)}) copy-start(u32[32]{0:T(128)} %constant.198) | copy-start | bytes 388
  10.8 13.8 %copy-start.16 = (s32[6]{0:T(128)S(1)}, s32[6]{0:T(128)}, u32[]{:S(2)}) copy-start(s32[6]{0:T(128)} %param.37) | copy-start | bytes 76
  10.8 65.1 %copy-start.11 = (f32[256,32]{0,1:T(8,128)S(1)}, f32[256,32]{0,1:T(8,128)}, u32[]{:S(2)}) copy-start(f32[256,32]{0,1:T(8,128)} %param.41) | copy-start | bytes 98308
  12.4 65.8 %copy-start.1 = (f32[1024,128]{1,0:T(8,128)S(1)}, f32[1024,128]{1,0:T(8,128)}, u32[]{:S(2)}) copy-start(f32[1024,128]{1,0:T(8,128)} %param.43) | copy-start | bytes 1572868
  16.0 108.9 %all-to-all-start.1 = ((f32[16,8,6]{1,2,0:T(8,128)}), f32[16,8,6]{1,2,0:T(8,128)S(1)}, u32[]{:S(2)}, u32[]{:S(2)}) async-start(f32[16,8,6]{1,2,0:T(8,128)} %copy.244), calls=%async_computation.1 | async-start | bytes 131072 | tf_op jit(solution)/shard_map/all_to_all | solution.py:117
  113.3 11.0 %copy-start.3 = (f32[6,96,128]{2,1,0:T(8,128)S(1)}, f32[6,96,128]{2,1,0:T(8,128)}, u32[]{:S(2)}) copy-start(f32[6,96,128]{2,1,0:T(8,128)} %param.35) | copy-start | bytes 884740
  124.5 5.1 %copy-start.14 = (f32[128,4]{0,1:T(4,128)S(1)}, f32[128,4]{0,1:T(4,128)}, u32[]{:S(2)}) copy-start(f32[128,4]{0,1:T(4,128)} %param.45) | copy-start | bytes 6148
  124.8 38.5 %copy-start.7 = (f32[4,128,128]{2,1,0:T(8,128)S(1)}, f32[4,128,128]{2,1,0:T(8,128)}, u32[]{:S(2)}) copy-start(f32[4,128,128]{2,1,0:T(8,128)} %param.44) | copy-start | bytes 786436
  124.9 40.2 %all-to-all-start = ((f32[128,6,256]{2,1,0:T(8,128)}), f32[128,6,256]{2,1,0:T(8,128)}, u32[]{:S(2)}, u32[]{:S(2)}) async-start(f32[128,6,256]{2,1,0:T(8,128)} %fusion.80), calls=%async_computation | async-start | bytes 2097152 | tf_op jit(solution)/shard_map/all_to_all | solution.py:116
  163.4 7.4 %copy-start.13 = (f32[128,8]{0,1:T(8,128)S(1)}, f32[128,8]{0,1:T(8,128)}, u32[]{:S(2)}) copy-start(f32[128,8]{0,1:T(8,128)} %param.40) | copy-start | bytes 12292
  165.1 102.8 %all-to-all-start.3 = ((f32[6,96,128]{2,0,1:T(8,128)}), f32[6,96,128]{2,0,1:T(8,128)S(1)}, u32[]{:S(2)}, u32[]{:S(2)}) async-start(f32[6,96,128]{2,0,1:T(8,128)} %fusion.85), calls=%async_computation.3 | async-start | bytes 786432 | tf_op jit(solution)/shard_map/all_to_all | solution.py:188
  214.3 1.2 copy-start.6
  224.3 39.1 %copy-start.8 = (f32[256,256]{1,0:T(8,128)S(1)}, f32[256,256]{1,0:T(8,128)}, u32[]{:S(2)}) copy-start(f32[256,256]{1,0:T(8,128)} %get-tuple-element.359) | copy-start | bytes 786436 | tf_op jit(solution)/shard_map/cond
  266.5 5.1 %copy-start.15 = (f32[128,4]{0,1:T(4,128)S(1)}, f32[128,4]{0,1:T(4,128)}, u32[]{:S(2)}) copy-start(f32[128,4]{0,1:T(4,128)} %param.48) | copy-start | bytes 6148
  267.9 35.1 %copy-start.10 = (f32[128,128]{1,0:T(8,128)S(1)}, f32[128,128]{1,0:T(8,128)}, u32[]{:S(2)}) copy-start(f32[128,128]{1,0:T(8,128)} %param.49) | copy-start | bytes 196612
  267.9 36.4 %all-to-all-start.2 = ((f32[8,96,256]{2,0,1:T(8,128)}), f32[8,96,256]{2,0,1:T(8,128)S(1)}, u32[]{:S(2)}, u32[]{:S(2)}) async-start(f32[8,96,256]{2,0,1:T(8,128)} %copy.248), calls=%async_computation.2 | async-start | bytes 1572864 | tf_op jit(solution)/shard_map/all_to_all | solution.py:144
  304.3 16.5 %all-to-all-start.4 = ((f32[96,6,128]{2,1,0:T(8,128)}), f32[96,6,128]{2,1,0:T(8,128)S(1)}, u32[]{:S(2)}, u32[]{:S(2)}) async-start(f32[96,6,128]{2,1,0:T(8,128)} %copy.262), calls=%async_computation.4 | async-start | bytes 786432 | tf_op jit(solution)/shard_map/all_to_all | solution.py:217
  308.7 0.9 copy-start.4
  309.7 11.5 %copy-start.5 = (f32[128,6,256]{2,0,1:T(8,128)S(1)}, f32[128,6,256]{2,0,1:T(8,128)}, u32[]{:S(2)}) copy-start(f32[128,6,256]{2,0,1:T(8,128)} %copy-done.4) | copy-start | bytes 2359300
  309.7 11.5 %collective-permute-start = (f32[64,6,256]{2,0,1:T(8,128)S(1)}, f32[64,6,256]{2,0,1:T(8,128)S(1)}, u32[]{:S(2)}, u32[]{:S(2)}) collective-permute-start(f32[64,6,256]{2,0,1:T(8,128)S(1)} %slice.53), channel_id=1, source_target_pairs={{0,16},{16,0},{1,17},{17,1},{2,18},{18,2},{3,19},{19,3},{4,20},{20... | collective-permute-start | bytes 1179656 | tf_op jit(solution)/shard_map/ppermute | solution.py:26
  320.9 9.1 %collective-permute-start.1 = (f32[6,96,64]{2,1,0:T(8,128)S(1)}, f32[6,96,64]{2,1,0:T(8,128)S(1)}, u32[]{:S(2)}, u32[]{:S(2)}) collective-permute-start(f32[6,96,64]{2,1,0:T(8,128)S(1)} %bitcast.269), channel_id=1, source_target_pairs={{0,16},{16,0},{1,17},{17,1},{2,18},{18,2},{3,19},{19,3},{4,20},{20... | collective-permute-start | bytes 442376 | tf_op jit(solution)/shard_map/ppermute | solution.py:26
Sparse Core Ops, SparseCore 0:
  15.4 42.3 all-gather.4
